TPU v7x, 512 devices: a whole 4x4x16 slice. The times are simulated.
512 devices in a mesh: slab: 128 (over z, y, core), rock: 4 (over x).
Axes of the slice: x: 4, y: 4, z: 16, core: 2. Of those that a mesh axis runs over, the one named last changes fastest.
Arguments:
- strain: float32 [16384, 6, 2048], P('slab', None, 'rock'), may hold values from -6 to 6
- dest: int32 [2, 16384, 1], P(None, 'slab'), may hold values from 0 to 127; in each aligned block of 128 rows (0 to 127, 128 to 255, ..., all dimensions but the last counted through in order) at most 2 rows name the same one
- det_row: int32 [2, 16384], P(None, 'slab'), may hold values from 0 to 7
- dirs: float32 [2, 4, 6], replicated, may hold values from -2.5 to 2.5
- rock_angles: float32 [16], replicated, may hold values from -2 to 2
- resolution: bfloat16 [2048, 2048], P(None, 'rock'), may hold values from -0.125 to 0.125
Outputs:
- detector: float32 [2, 1024, 16, 2048], P(None, 'slab', None, 'rock')
Inputs may be any that keep to these rules, and one draw needn't show every extreme that they name: `dest`: within the 128 tiles of one index of slab, at one angle, at most 2 tiles name the same owner, a bound that some block reaches.
All inputs are finite; a program needn't handle non-finite values.
Results may differ from a plain program's by a relative error of at most 0.0003.
Values sent between devices are 32-bit elements; how exact they have to be, the bound alone decides.
A program may use at most 128 MiB of HBM per device.

v0:
```python
import jax
import jax.numpy as jnp
from jax import lax
from jax.sharding import PartitionSpec as P

TILES_DEV = 128
DEPTH = 1
QDIR = 4
ROWS = 8
ANGLES = 2


def sent_together(arrays, axis, split_dim, concat_dim, along):
    columns = [a.reshape(*a.shape[:along], -1) for a in arrays]
    both = jnp.concatenate(columns, axis=along)
    filled, at, finished = (
        lax.all_to_all(both, axis, split_axis=split_dim, concat_axis=concat_dim, tiled=True),
        0,
        [],
    )
    for a, column in zip(arrays, columns):
        slab = filled[..., at : at + column.shape[along]]
        finished.append(slab.reshape(*slab.shape[:along], *a.shape[along:]))
        at += column.shape[along]
    return tuple(finished)


def joined_along(pieces, dim):
    pieces = jnp.moveaxis(pieces, 0, dim)
    dims = pieces.shape
    return pieces.reshape(*dims[:dim], dims[dim] * dims[dim + 1], *dims[dim + 2 :])


def copy_for_each(array, axis):
    copies = jnp.broadcast_to(array, (lax.axis_size(axis), *array.shape))
    return lax.all_to_all(copies, axis, split_axis=0, concat_axis=0, tiled=True)


def collect(array, axis, dim):
    return joined_along(copy_for_each(array, axis), dim)


def local(strain, dest, det_row, dirs, rock_angles, resolution):
    slabs = lax.axis_size("slab")
    tiles_here = strain.shape[0]
    vox_here = strain.shape[2]
    pix_here = resolution.shape[1]
    depth = vox_here // pix_here
    capacity = 2 * tiles_here // slabs
    slots = slabs * capacity
    block_size = 64
    rocks = rock_angles.shape[0]
    qcount = dirs.shape[1]
    norm = ROWS / (QDIR * DEPTH * TILES_DEV)
    row_ids = jnp.arange(ROWS, dtype=jnp.float32)
    lower = lax.broadcasted_iota(jnp.int32, (tiles_here, tiles_here), 1) < lax.broadcasted_iota(
        jnp.int32, (tiles_here, tiles_here), 0
    )

    def add_block(total, item):
        proj_block, row_block = item
        inten = jnp.sum(
            jnp.exp(-0.5 * (proj_block[:, :, None, :] - rock_angles[None, None, :, None]) ** 2),
            axis=1,
        )
        summed = inten.reshape(block_size, rocks, pix_here, depth).sum(axis=3)
        onehot = (row_ids[:, None] == row_block[None, :]).astype(jnp.float32)
        added = jnp.dot(
            onehot, summed.reshape(block_size, rocks * pix_here), precision=lax.Precision.HIGHEST
        )
        return (total + added, None)

    images = []
    for angle in range(ANGLES):
        owner = dest[angle, :, 0]
        same = (owner[:, None] == owner[None, :]) & lower
        rank = jnp.sum(same.astype(jnp.int32), axis=1)
        slot = owner * capacity + rank
        row_send = (
            jnp.full((slots,), -1.0, jnp.float32).at[slot].set(det_row[angle].astype(jnp.float32))
        )
        row_send = row_send.reshape(slabs, capacity)
        weights = dirs[angle]
        local_proj = jnp.einsum("qc,tcv->tqv", weights, strain, precision=lax.Precision.HIGHEST)
        outgoing = jnp.zeros((slots, qcount, vox_here), jnp.float32).at[slot].set(local_proj)
        outgoing = outgoing.reshape(slabs, capacity, qcount, vox_here)
        arrived, arrived_rows = sent_together((outgoing, row_send), "slab", 0, 0, 2)
        proj = arrived.reshape(slots, qcount, vox_here)
        proj_blocks = proj.reshape(slots // block_size, block_size, qcount, vox_here)
        row_blocks = arrived_rows.reshape(slots // block_size, block_size)
        image, unused = lax.scan(
            add_block, jnp.zeros((ROWS, rocks * pix_here), jnp.float32), (proj_blocks, row_blocks)
        )
        images.append(image.reshape(ROWS, rocks, pix_here) * norm)
    stacked = jnp.stack(images, axis=0)
    columns = resolution.astype(jnp.float32)
    return jnp.einsum(
        "agrp,pk->agrk", collect(stacked, "rock", 3), columns, precision=lax.Precision.HIGHEST
    )


def solution(mesh):
    placed = (
        P("slab", None, "rock"),
        P(None, "slab", None),
        P(None, "slab"),
        P(),
        P(),
        P(None, "rock"),
    )
    return jax.shard_map(
        local, mesh=mesh, in_specs=placed, out_specs=P(None, "slab", None, "rock"), check_vma=False
    )
```

profile of v0, /device:TPU:24, one launch (start us, length us, event | category | flops | bytes accessed | tf_op | source)
XLA Modules:
  0.0 342.5 jit_solution(9741041165035415520)
XLA Ops:
  3.7 4.2 %fusion.12 = f32[128,4,512]{2,1,0:T(4,128)S(1)} fusion(f32[128,6,512]{2,0,1:T(8,128)} %param.10, f32[2,4,6]{2,1,0:T(4,128)} %param.13), kind=kOutput, calls=%fused_computation.26 | convolution fusion | flops 18874368 | bytes 2623488 | tf_op jit(solution)/shard_map/qc,tcv->tqv/dot_general | solution.py:84
  9.5 13.7 %scatter_fusion = f32[256,4,512]{2,1,0:T(4,128)} fusion(f32[256,4,512]{2,1,0:T(4,128)} %broadcast.94.clone.1, s32[128]{0:T(128)S(1)} %get-tuple-element.133, f32[128,4,512]{2,1,0:T(4,128)S(1)} %fusion.12), kind=kCustom, calls=%fused_computation | custom fusion | bytes 3146240 | tf_op jit(solution)/shard_map/scatter | solution.py:85
  23.2 4.4 %reshape_reshape.18 = f32[128,2,2048]{2,1,0:T(2,128)} reshape(f32[256,4,512]{2,1,0:T(4,128)} %scatter_fusion) | data formatting | bytes 4194304 | tf_op jit(solution)/shard_map/reshape;reshape | solution.py:14
  27.5 4.1 %pad_maximum_fusion = f32[128,2,2049]{2,1,0:T(2,128)} fusion(f32[128,2,1]{2,1,0:T(2,128)S(1)} %reshape_reshape.24, f32[128,2,2048]{2,1,0:T(2,128)} %reshape_reshape.18), kind=kLoop, calls=%fused_computation.22 | loop fusion | flops 524544 | bytes 4196352 | tf_op jit(solution)/shard_map/concatenate | solution.py:15
  31.7 19.8 %all-to-all-start = ((f32[128,2,2049]{2,1,0:T(2,128)}), f32[128,2,2049]{2,1,0:T(2,128)}, u32[]{:S(2)}, u32[]{:S(2)}) async-start(f32[128,2,2049]{2,1,0:T(2,128)} %pad_maximum_fusion), calls=%async_computation | async-start | bytes 4456448 | tf_op jit(solution)/shard_map/all_to_all | solution.py:17
  52.9 4.2 %fusion.15 = f32[128,4,512]{2,1,0:T(4,128)S(1)} fusion(f32[128,6,512]{2,0,1:T(8,128)} %param.10, f32[2,4,6]{2,1,0:T(4,128)S(1)} %copy-done.1), kind=kOutput, calls=%fused_computation.27 | convolution fusion | flops 18874368 | bytes 2623488 | tf_op jit(solution)/shard_map/qc,tcv->tqv/dot_general | solution.py:84
  58.7 13.7 %scatter_fusion.1 = f32[256,4,512]{2,1,0:T(4,128)} fusion(f32[256,4,512]{2,1,0:T(4,128)} %broadcast.94.clone, s32[128]{0:T(128)S(1)} %get-tuple-element.134, f32[128,4,512]{2,1,0:T(4,128)S(1)} %fusion.15), kind=kCustom, calls=%fused_computation.2 | custom fusion | bytes 3146240 | tf_op jit(solution)/shard_map/scatter | solution.py:85
  72.4 4.4 %reshape_reshape.21 = f32[128,2,2048]{2,1,0:T(2,128)} reshape(f32[256,4,512]{2,1,0:T(4,128)} %scatter_fusion.1) | data formatting | bytes 4194304 | tf_op jit(solution)/shard_map/reshape;reshape | solution.py:14
  76.8 4.1 %pad_maximum_fusion.1 = f32[128,2,2049]{2,1,0:T(2,128)} fusion(f32[128,2,1]{2,1,0:T(2,128)S(1)} %reshape_reshape.25, f32[128,2,2048]{2,1,0:T(2,128)} %reshape_reshape.21), kind=kLoop, calls=%fused_computation.23 | loop fusion | flops 524544 | bytes 4196352 | tf_op jit(solution)/shard_map/concatenate | solution.py:15
  80.9 72.5 %all-to-all-done = f32[128,2,2049]{2,1,0:T(2,128)} async-done(((f32[128,2,2049]{2,1,0:T(2,128)}), f32[128,2,2049]{2,1,0:T(2,128)}, u32[]{:S(2)}, u32[]{:S(2)}) %all-to-all-start) | async-done | bytes 2098208 | tf_op jit(solution)/shard_map/all_to_all | solution.py:17
  153.5 10.7 %all-to-all-start.1 = ((f32[128,2,2049]{2,1,0:T(2,128)}), f32[128,2,2049]{2,1,0:T(2,128)}, u32[]{:S(2)}, u32[]{:S(2)}) async-start(f32[128,2,2049]{2,1,0:T(2,128)} %pad_maximum_fusion.1), calls=%async_computation.1 | async-start | bytes 4456448 | tf_op jit(solution)/shard_map/all_to_all | solution.py:17
  164.2 3.2 slice.41
  167.4 4.5 %reshape_reshape_reshape.6 = f32[4,64,4,512]{3,2,1,0:T(4,128)} reshape(f32[128,2,2048]{2,1,0:T(2,128)} %slice.41) | data formatting | bytes 4194304 | tf_op jit(solution)/shard_map/reshape;reshape;reshape | solution.py:89
  173.1 32.8 %while.22 = (s32[]{:T(128)}, f32[8,8192]{1,0:T(8,128)S(1)}, f32[4,64]{1,0:T(4,128)S(1)}, f32[4,64,4,512]{3,2,1,0:T(4,128)}, f32[16]{0:T(128)S(1)}, /*index=5*/s32[]{:T(128)}, s32[]{:T(128)}) while((s32[]{:T(128)}, f32[8,8192]{1,0:T(8,128)S(1)}, f32[4,64]{1,0:T(4,128)S(1)}, f32[4,64,4,512]{3,2,1,0:T(4,128)}, f32[16]{0:T(128)S(1)}, ...), condition=%wide.region_5.6_spmd.clone, body=%wide.region_3.5_spmd.clone.sunk | while | flops 58327552 | bytes 10486687 | solution.py:91
  176.3 2.5 copy.49
  178.9 2.4 convolution_add_fusion.4
  184.5 2.5 copy.49
  192.7 2.5 copy.49
  195.3 2.4 convolution_add_fusion.4
  200.9 2.5 copy.49
  206.0 60.1 %all-to-all-done.1 = f32[128,2,2049]{2,1,0:T(2,128)} async-done(((f32[128,2,2049]{2,1,0:T(2,128)}), f32[128,2,2049]{2,1,0:T(2,128)}, u32[]{:S(2)}, u32[]{:S(2)}) %all-to-all-start.1) | async-done | bytes 2098208 | tf_op jit(solution)/shard_map/all_to_all | solution.py:17
  266.1 3.1 slice.43
  269.2 4.4 %reshape_reshape_reshape.7 = f32[4,64,4,512]{3,2,1,0:T(4,128)} reshape(f32[128,2,2048]{2,1,0:T(2,128)} %slice.43) | data formatting | bytes 4194304 | tf_op jit(solution)/shard_map/reshape;reshape;reshape | solution.py:89
  274.8 32.8 %while.23 = (s32[]{:T(128)}, f32[8,8192]{1,0:T(8,128)S(1)}, f32[4,64]{1,0:T(4,128)S(1)}, f32[4,64,4,512]{3,2,1,0:T(4,128)}, f32[16]{0:T(128)S(1)}, /*index=5*/s32[]{:T(128)}, s32[]{:T(128)}) while((s32[]{:T(128)}, f32[8,8192]{1,0:T(8,128)S(1)}, f32[4,64]{1,0:T(4,128)S(1)}, f32[4,64,4,512]{3,2,1,0:T(4,128)}, f32[16]{0:T(128)S(1)}, ...), condition=%wide.region_11.12_spmd.clone, body=%wide.region_9.11_spmd.clone.sunk | while | flops 58327552 | bytes 10486687 | solution.py:91
  278.1 2.5 copy.50
  286.3 2.5 copy.50
  294.5 2.5 copy.50
  297.1 2.4 convolution_add_fusion.5
  302.7 2.5 copy.50
  305.3 2.4 convolution_add_fusion.5
  308.2 31.4 %all_to_all.15 = f32[4,2,8,16,512]{4,3,2,1,0:T(8,128)S(1)} all-to-all(f32[4,2,8,16,512]{4,3,2,1,0:T(8,128)S(1)} %broadcast_in_dim.2), channel_id=1, replica_groups=mesh['slab'=128,'rock'=4] {'rock'}, dimensions={0} | all-to-all | bytes 4194304 | tf_op jit(solution)/shard_map/all_to_all | solution.py:36
  339.9 2.6 fusion.10
  (57 shorter events, 47.2 us)
Async XLA Ops:
  0.0 339.9 %copy-start = (bf16[2048,512]{1,0:T(8,128)(2,1)S(1)}, bf16[2048,512]{1,0:T(8,128)(2,1)}, u32[]{:S(2)}) copy-start(bf16[2048,512]{1,0:T(8,128)(2,1)} %param.15) | copy-start | bytes 6291460
  31.7 21.3 %copy-start.1 = (f32[2,4,6]{2,1,0:T(4,128)S(1)}, f32[2,4,6]{2,1,0:T(4,128)}, u32[]{:S(2)}) copy-start(f32[2,4,6]{2,1,0:T(4,128)} %param.13) | copy-start | bytes 580
  31.7 121.8 %all-to-all-start = ((f32[128,2,2049]{2,1,0:T(2,128)}), f32[128,2,2049]{2,1,0:T(2,128)}, u32[]{:S(2)}, u32[]{:S(2)}) async-start(f32[128,2,2049]{2,1,0:T(2,128)} %pad_maximum_fusion), calls=%async_computation | async-start | bytes 4456448 | tf_op jit(solution)/shard_map/all_to_all | solution.py:17
  153.5 112.7 %all-to-all-start.1 = ((f32[128,2,2049]{2,1,0:T(2,128)}), f32[128,2,2049]{2,1,0:T(2,128)}, u32[]{:S(2)}, u32[]{:S(2)}) async-start(f32[128,2,2049]{2,1,0:T(2,128)} %pad_maximum_fusion.1), calls=%async_computation.1 | async-start | bytes 4456448 | tf_op jit(solution)/shard_map/all_to_all | solution.py:17
  167.4 5.7 %copy-start.2 = (f32[16]{0:T(128)S(1)}, f32[16]{0:T(128)}, u32[]{:S(2)}) copy-start(f32[16]{0:T(128)} %param.14) | copy-start | bytes 196
where the time goes:
time: 346 us; the launch traced here: 343 us
  waiting for transfers between devices  133 us (38%)
  local copies, waits for them, and re-layouts  90.3 us (26%)
  blocking collectives  31.4 us (9%)
  starting transfers between devices  30.5 us (9%)
  matrix products  29.9 us (9%)
  other arithmetic  27.4 us (8%)
    all_to_all x2, waiting for transfers between devices, sent_together(): lax.all_to_all(both, axis, split_axis=split_dim, concat_axis=concat_dim,...  133 us
    all_to_all x1, blocking collectives, copy_for_each(): return lax.all_to_all(copies, axis, split_axis=0, concat_axis=0, tiled=True)  31.4 us
    all_to_all x2, starting transfers between devices, sent_together(): lax.all_to_all(both, axis, split_axis=split_dim, concat_axis=concat_dim,...  30.5 us
    scatter x2, local copies, waits for them, and re-layouts, local(): jnp.zeros((slots, qcount, vox_here), jnp.float32).at[slot].set(local_proj)  27.4 us
    while x8, local copies, waits for them, and re-layouts  20.3 us
    dot_general x8, matrix products, add_block(): jnp.dot(onehot, summed.reshape(block_size, rocks * pix_here), precision=l...  18.9 us
    reduce_sum x8, other arithmetic, add_block(): jnp.sum(jnp.exp(-0.5 * (proj_block[:, :, None, :] - rock_angles[None, Non...  17.5 us
    another operation x4, local copies, waits for them, and re-layouts, sent_together(): columns = [a.reshape(*a.shape[:along], -1) for a in arrays]  9.31 us
  transfers between devices with their start and end apart: 2, of which 2 were waited for; matrix products, arithmetic and copies ran while one was open for 21% of the time, Pallas kernels for 0%

commit v1 on v0

v1 whole, which is shorter than its diff:
```python
import functools
import math

import jax
import jax.numpy as jnp
from jax import lax
from jax.experimental import pallas as pl
from jax.experimental.pallas import tpu as pltpu
from jax.sharding import PartitionSpec as P

TILES_DEV = 128
DEPTH = 1
QDIR = 4
ROWS = 8
ANGLES = 2
CAP = 2
PLANE = 8
GROUPS = 4
MESH = pl.DeviceIdType.MESH


def kernel(
    nz, nd, nx,
    idx, cr, post, w, strain, res, oh, out,
    ysend, yrecv, ohrecv, ohm, zfirst, zrecv, ximg,
    oh_ss, oh_rs, y_ss, y_rs, z_ss, z_rs, x_ss, x_rs,
):
    me = lax.axis_index("slab")
    x = lax.axis_index("rock")
    z = lax.div(me, nd)
    d = lax.rem(me, nd)
    half = nz // 2
    owners = nz * nd
    px = strain.shape[2]
    per = zfirst.shape[2]
    lanes = w.shape[3]

    def plane(k):
        return {"slab": z * nd + lax.rem(d + k, nd)}

    def ring(step):
        return {"slab": lax.rem(z + step + nz, nz) * nd + d}

    def across(k):
        return {"rock": lax.rem(x + k, nx)}

    peers = [plane(k) for k in range(1, nd)] + [ring(1), ring(-1)] + [across(k) for k in range(1, nx)]
    barrier = pltpu.get_barrier_semaphore()
    for peer in peers:
        pl.semaphore_signal(barrier, inc=1, device_id=peer, device_id_type=MESH)
    pl.semaphore_wait(barrier, len(peers))

    def remote(src, dst, ss, rs, peer):
        return pltpu.make_async_remote_copy(
            src_ref=src, dst_ref=dst, send_sem=ss, recv_sem=rs, device_id=peer, device_id_type=MESH
        )

    def wait_bytes(ref, sem):
        pltpu.make_async_copy(ref, ref, sem).wait()

    def dest_z(m, sign):
        off = half - m
        if sign == 0:
            return lax.rem(z + off, nz)
        back = lax.rem(off, half)
        return lax.rem(z - back + nz, nz)

    for k in range(1, nd):
        remote(oh.at[lax.rem(d + k, nd)], ohrecv.at[d], oh_ss, oh_rs, plane(k)).start()
    ohrecv[d] = oh[d]

    upper = lax.broadcasted_iota(jnp.int32, (2 * QDIR, lanes), 0) < QDIR

    def pair(a, owner, put):
        base = (a * owners + owner) * CAP
        first, second = idx[base], idx[base + 1]
        for lb in range(px // lanes):
            cols = pl.ds(lb * lanes, lanes)
            total = None
            for c in range(w.shape[1]):
                s0 = jnp.broadcast_to(strain[first, pl.ds(c, 1), cols], upper.shape)
                s1 = jnp.broadcast_to(strain[second, pl.ds(c, 1), cols], upper.shape)
                term = w[a, c] * jnp.where(upper, s0, s1)
                total = term if total is None else total + term
            put(cols, total)

    def send_group(a, m):
        def one(k, carry):
            dk = lax.rem(d + k, nd)
            for sign in range(2):
                owner = dest_z(m, sign) * nd + dk

                def put(cols, value, sign=sign):
                    ysend[a, m, k - 1, sign, :, cols] = value

                pair(a, owner, put)
            remote(
                ysend.at[a, m, k - 1], yrecv.at[a, m, d], y_ss.at[a, m], y_rs.at[a, m], plane(k)
            ).start()
            return carry

        lax.fori_loop(1, nd, one, 0)
        for sign in range(2):

            def put(cols, value, sign=sign):
                yrecv[a, m, d, sign, :, cols] = value

            pair(a, dest_z(m, sign) * nd + d, put)

    def need_group(a, m):
        wait_bytes(yrecv.at[a, m, pl.ds(0, nd - 1)], y_rs.at[a, m])

    def work(a, m, sign, r):
        zd = dest_z(m, sign)
        p = yrecv[a, m, :, sign].reshape(nd * 2 * QDIR, px)
        e = jnp.exp2(p * (cr[r] - p))
        hi = e.astype(jnp.bfloat16)
        lo = (e - hi.astype(jnp.float32)).astype(jnp.bfloat16)
        lhs = ohm[a, pl.ds(pl.multiple_of(zd * ROWS, ROWS), ROWS), :].astype(jnp.bfloat16)
        return jnp.dot(lhs, jnp.concatenate([hi, lo], axis=0), preferred_element_type=jnp.float32)

    def z_step(a, m, g, way, has):
        here = zrecv.at[a, m - 1, way, g]
        if has:
            wait_bytes(here, z_rs.at[a, m - 1, way, g])

        def one(i, carry):
            value = work(a, m, way, g * per + i)
            if has:
                value = value + here[i]
            here[i] = value
            return carry

        lax.fori_loop(0, per, one, 0)
        remote(
            here, zrecv.at[a, m, way, g], z_ss.at[a, m, way, g], z_rs.at[a, m, way, g], ring(1 - 2 * way)
        ).start()

    def z_first(a):
        for way in range(2):

            def go(g, carry):
                def one(i, inner):
                    zfirst[a, g, i] = work(a, 0, 0, g * per + i)
                    return inner

                lax.fori_loop(0, per, one, 0)
                remote(
                    zfirst.at[a, g], zrecv.at[a, 0, way, g], z_ss.at[a, 0, way, g], z_rs.at[a, 0, way, g],
                    ring(1 - 2 * way),
                ).start()
                return carry

            lax.fori_loop(way * GROUPS // 2, (way + 1) * GROUPS // 2, go, 0)

    def z_second(a):
        for has in (True, False):

            def go(i, carry):
                for way in range(2):
                    g = i + (way if has else 1 - way) * (GROUPS // 2)
                    z_step(a, 1, g, way, has)
                return carry

            lax.fori_loop(0, GROUPS // 2, go, 0)

    def z_rest(a, m):
        def go(g, carry):
            for way in range(2):
                z_step(a, m, g, way, True)
            return carry

        lax.fori_loop(0, GROUPS, go, 0)

    def finish(a):
        def go(g, carry):
            for way in range(2):
                wait_bytes(zrecv.at[a, half - 1, way, g], z_rs.at[a, half - 1, way, g])

            def one(i, inner):
                r = g * per + i
                value = work(a, 0, 1, r) + zrecv[a, half - 1, 0, g, i] + zrecv[a, half - 1, 1, g, i]
                ximg[a, g, x, i] = value * post[r]
                return inner

            lax.fori_loop(0, per, one, 0)
            for k in range(1, nx):
                remote(ximg.at[a, g, x], ximg.at[a, g, x], x_ss.at[a, g], x_rs.at[a, g], across(k)).start()
            return carry

        lax.fori_loop(0, GROUPS, go, 0)

    def resolve(a):
        def go(g, carry):
            wait_bytes(ximg.at[a, g, pl.ds(0, nx - 1)], x_rs.at[a, g])
            total = None
            for j in range(nx):
                image = ximg[a, g, j].reshape(per * ROWS, px)
                hi = image.astype(jnp.bfloat16)
                lo = (image - hi.astype(jnp.float32)).astype(jnp.bfloat16)
                both = jnp.dot(
                    jnp.concatenate([hi, lo], axis=0), res[pl.ds(j * px, px), :], preferred_element_type=jnp.float32
                )
                part = both[: per * ROWS] + both[per * ROWS :]
                total = part if total is None else total + part
            out[a, pl.ds(g * per, per)] = total.reshape(per, ROWS, res.shape[1])
            return carry

        lax.fori_loop(0, GROUPS, go, 0)

    lead = 2
    units = [(a, m) for a in range(ANGLES) for m in range(half)]
    for a, m in units[:lead]:
        send_group(a, m)
    wait_bytes(ohrecv.at[pl.ds(0, nd - 1)], oh_rs)
    for a in range(ANGLES):
        columns = ohrecv[:, a].reshape(nd * 2 * QDIR, nz * ROWS)
        rows = columns.T
        ohm[a] = jnp.concatenate([rows, rows], axis=1)

    def steady(a):
        def go(m, carry):
            ahead = a * half + m + lead
            @pl.when(ahead < ANGLES * half)
            def _():
                send_group(lax.div(ahead, half), lax.rem(ahead, half))
            need_group(a, m)
            z_rest(a, m)
            return carry

        return go

    for a in range(ANGLES):
        for m in range(2):
            ahead = a * half + m + lead
            if ahead < ANGLES * half:
                send_group(ahead // half, ahead % half)
            need_group(a, m)
            (z_first if m == 0 else z_second)(a)
        if a > 0:
            finish(a - 1)
        if half > 2:
            lax.fori_loop(2, half, steady(a), 0)
        if a > 0:
            resolve(a - 1)
    finish(ANGLES - 1)
    resolve(ANGLES - 1)

    wait_bytes(ohrecv.at[pl.ds(0, nd - 1)], oh_ss)
    for a in range(ANGLES):

        def drain(m, carry):
            wait_bytes(ysend.at[a, m, pl.ds(0, nd - 1)], y_ss.at[a, m])
            return carry

        lax.fori_loop(0, half, drain, 0)

        def drain_z(m, carry):
            for way in range(2):
                for g in range(GROUPS):
                    wait_bytes(zrecv.at[a, m, way, g], z_ss.at[a, m, way, g])
            return carry

        for way in range(2):
            for g in range(way * GROUPS // 2, (way + 1) * GROUPS // 2):
                wait_bytes(zrecv.at[a, 0, way, g], z_ss.at[a, 0, way, g])
        lax.fori_loop(1, half, drain_z, 0)
        for g in range(GROUPS):
            wait_bytes(ximg.at[a, g, pl.ds(0, nx - 1)], x_ss.at[a, g])


def local(plane, strain, dest, det_row, dirs, rock_angles, resolution):
    nslab, nx = lax.axis_size("slab"), lax.axis_size("rock")
    nd, nz = plane, nslab // plane
    half = nz // 2
    tiles, comps, px = strain.shape
    out_px = resolution.shape[1]
    rocks = rock_angles.shape[0]
    per = rocks // GROUPS
    lanes = min(128, px)
    norm = ROWS / (QDIR * DEPTH * TILES_DEV)
    scale = math.sqrt(0.5 * math.log2(math.e))

    key = jnp.arange(tiles, dtype=jnp.int32)[None, :] * ROWS + det_row
    match = dest == jnp.arange(nslab, dtype=jnp.int32)[None, None, :]
    lowest = jnp.min(jnp.where(match, key[:, :, None], tiles * ROWS), axis=1)
    highest = jnp.max(jnp.where(match, key[:, :, None], -1), axis=1)
    keys = jnp.stack([jnp.where(highest >= 0, lowest, -1), jnp.where(highest > lowest, highest, -1)], axis=-1)
    idx = jnp.maximum(keys, 0) // ROWS
    rows = jnp.where(keys >= 0, keys % ROWS, -1)
    rows = jnp.transpose(rows.reshape(ANGLES, nz, nd, CAP), (2, 0, 3, 1))
    hot = rows[:, :, :, None, :, None] == jnp.arange(ROWS, dtype=jnp.int32)
    oh = jnp.broadcast_to(hot, (nd, ANGLES, CAP, QDIR, nz, ROWS)).astype(jnp.float32)
    oh = oh.reshape(nd, ANGLES, CAP * QDIR, nz * ROWS)

    w = jnp.transpose(dirs, (0, 2, 1)) * scale
    w = jnp.concatenate([w, w], axis=2)
    w = jnp.broadcast_to(w[..., None], (ANGLES, comps, 2 * QDIR, lanes))
    angles = rock_angles * scale
    cr = 2.0 * angles
    post = norm * jnp.exp2(-angles * angles)

    smem = pl.BlockSpec(memory_space=pltpu.SMEM)
    vmem = pl.BlockSpec(memory_space=pltpu.VMEM)
    dma = pltpu.SemaphoreType.DMA
    f32 = jnp.float32
    image = (per, ROWS, px)
    resolved = pl.pallas_call(
        functools.partial(kernel, nz, nd, nx),
        out_shape=jax.ShapeDtypeStruct((ANGLES, rocks, ROWS, out_px), f32),
        in_specs=[smem, smem, smem, vmem, vmem, vmem, vmem],
        out_specs=vmem,
        scratch_shapes=[
            pltpu.VMEM((ANGLES, half, nd - 1, 2, 2 * QDIR, px), f32),
            pltpu.VMEM((ANGLES, half, nd, 2, 2 * QDIR, px), f32),
            pltpu.VMEM((nd, ANGLES, CAP * QDIR, nz * ROWS), f32),
            pltpu.VMEM((ANGLES, nz * ROWS, 2 * nd * 2 * QDIR), f32),
            pltpu.VMEM((ANGLES, GROUPS, *image), f32),
            pltpu.VMEM((ANGLES, half, 2, GROUPS, *image), f32),
            pltpu.VMEM((ANGLES, GROUPS, nx, *image), f32),
            dma,
            dma,
            dma((ANGLES, half)),
            dma((ANGLES, half)),
            dma((ANGLES, half, 2, GROUPS)),
            dma((ANGLES, half, 2, GROUPS)),
            dma((ANGLES, GROUPS)),
            dma((ANGLES, GROUPS)),
        ],
        compiler_params=pltpu.CompilerParams(collective_id=0, has_side_effects=True),
    )(idx.reshape(-1), cr, post, w, strain, resolution, oh)
    return jnp.swapaxes(resolved, 1, 2)


def solution(mesh):
    placed = (
        P("slab", None, "rock"),
        P(None, "slab", None),
        P(None, "slab"),
        P(),
        P(),
        P(None, "rock"),
    )
    return jax.shard_map(
        functools.partial(local, PLANE),
        mesh=mesh,
        in_specs=placed,
        out_specs=P(None, "slab", None, "rock"),
        check_vma=False,
    )
```

time: 346 us -> 143 us (0.41)
  waiting for transfers between devices: 133 us -> 0 us
  Pallas kernels: 0 us -> 131 us
  local copies, waits for them, and re-layouts: 90.3 us -> 7.24 us
  blocking collectives: 31.4 us -> 0 us
  starting transfers between devices: 30.5 us -> 0 us
  matrix products: 29.9 us -> 0 us
  other arithmetic: 27.4 us -> 4.36 us
    all_to_all x2 -> x0, waiting for transfers between devices: 133 us -> none  [sent_together(): lax.all_to_all(both, axis, split_axis=split_dim, concat_axis=concat_dim,...]
    pallas_call x0 -> x1, Pallas kernels: none -> 131 us  [local(): pl.pallas_call(functools.partial(kernel, nz, nd, nx), out_shape=jax.Shape...]
    all_to_all x1 -> x0, blocking collectives: 31.4 us -> none  [copy_for_each(): return lax.all_to_all(copies, axis, split_axis=0, concat_axis=0, tiled=True)]
    all_to_all x2 -> x0, starting transfers between devices: 30.5 us -> none  [sent_together(): lax.all_to_all(both, axis, split_axis=split_dim, concat_axis=concat_dim,...]
    dot_general x11 -> x0, matrix products: 29.9 us -> none  [the longest x8 18.9 us: add_block(): jnp.dot(onehot, summed.reshape(block_size, rocks * pix_here), precision=l...]
    scatter x4 -> x0, local copies, waits for them, and re-layouts: 29.6 us -> none  [the longest x2 27.4 us: local(): jnp.zeros((slots, qcount, vox_here), jnp.float32).at[slot].set(local_proj)]
    another operation x10 -> x0, local copies, waits for them, and re-layouts: 21.6 us -> none  [the longest x4 9.31 us: sent_together(): columns = [a.reshape(*a.shape[:along], -1) for a in arrays]]
    while x8 -> x0, local copies, waits for them, and re-layouts: 20.3 us -> none
  transfers between devices with their start and end apart: 2 -> 0, of which waited for: 2 -> 0; matrix products, arithmetic and copies ran while one was open for 21% -> 0% of each run, Pallas kernels for 0% -> 0%
where the time goes in v1:
time: 143 us
  Pallas kernels  131 us (92%)
  local copies, waits for them, and re-layouts  7.24 us (5%)
  other arithmetic  4.36 us (3%)
    pallas_call x1, Pallas kernels, local(): pl.pallas_call(functools.partial(kernel, nz, nd, nx), out_shape=jax.Shape...  131 us

profile of v1, /device:TPU:24, one launch (start us, length us, event | category | flops | bytes accessed | tf_op | source)
XLA Modules:
  0.0 142.8 jit_solution(14165072246437021286)
XLA Ops:
  0.0 0.0 copy-start
  0.0 0.8 broadcast_add_fusion
  0.8 0.8 select_reduce_fusion.1
  1.6 1.3 fusion.6
  2.9 0.7 multiply_bitcast_fusion
  3.6 0.1 copy.18
  3.7 0.1 reduce_max.15
  3.8 0.1 reduce_min.15
  3.9 0.1 copy.19
  4.0 0.2 copy.16
  4.2 0.2 and.18
  4.4 0.7 broadcast_in_dim.50.w
  5.1 0.1 copy.17
  5.2 0.1 div.12
  5.3 0.6 add_select_fusion.1.idx
  5.9 0.1 fusion
  6.1 0.1 broadcast_in_dim.53
  6.1 1.1 reshape.96.oh
  7.2 0.0 copy-done
  7.2 2.3 %copy.20.strain = f32[128,6,512]{2,1,0:T(8,128)} copy(f32[128,6,512]{2,0,1:T(8,128)S(1)} %copy-done) | data formatting | bytes 3145728 | tf_op args[0]
  9.5 131.1 %shard_map.64 = f32[2,16,8,512]{3,2,1,0:T(8,128)} custom-call(s32[512]{0:T(512)} %add_select_fusion.1.idx, f32[16]{0:T(128)} %get-tuple-element.12.cr, f32[16]{0:T(128)} %get-tuple-element.11.post, f32[2,6,8,128]{3,2,1,0:T(8,128)} %broadcast_in_dim.50.w, f32[128,6,512]{2,1,0:T(8,128)} %copy.20.strain, bf16[2048,512]{1,0:T(8,128)(2,1)} %res.1, ...), custom_call_target="tpu_custom_call" | custom-call | tf_op jit(solution)/shard_map/pallas_call | solution.py:308
  140.7 2.1 %copy.21 = f32[2,8,16,512]{3,2,1,0:T(8,128)} copy(f32[2,8,16,512]{3,1,2,0:T(8,128)} %bitcast.14) | data formatting | bytes 1048576 | tf_op jit(solution)/shard_map/transpose | solution.py:332
  (7 shorter events, 0.1 us)
Async XLA Ops:
  0.0 7.2 %copy-start = (f32[128,6,512]{2,0,1:T(8,128)S(1)}, f32[128,6,512]{2,0,1:T(8,128)}, u32[]{:S(2)}) copy-start(f32[128,6,512]{2,0,1:T(8,128)} %param.6) | copy-start | bytes 4718596

commit v2 on v1

v2 whole, which is shorter than its diff:
```python
import functools
import math

import jax
import jax.numpy as jnp
from jax import lax
from jax.experimental import pallas as pl
from jax.experimental.pallas import tpu as pltpu
from jax.sharding import PartitionSpec as P

TILES_DEV = 128
DEPTH = 1
QDIR = 4
ROWS = 8
ANGLES = 2
CAP = 2
PLANE = 8
GROUPS = 4
LEAD = 3
MESH = pl.DeviceIdType.MESH


def kernel(
    nz, nd, norm,
    ra, dirs, dest, det_row, strain_hbm, res_hbm, out,
    idx, idx_v, w, strain, res, oh, ysend, yrecv, ohrecv, ohm, zfirst, zrecv, ximg,
    load_s, idx_s, oh_ss, oh_rs, y_ss, y_rs, z_ss, z_rs, x_ss, x_rs,
):
    me = lax.axis_index("slab")
    x = lax.axis_index("rock")
    nx = 4
    z = lax.div(me, nd)
    d = lax.rem(me, nd)
    half = nz // 2
    owners = nz * nd
    comps, blocks, tiles, lanes = strain.shape
    px = blocks * lanes
    per = zfirst.shape[2]
    scale = math.sqrt(0.5 * math.log2(math.e))
    f32, i32, bf16 = jnp.float32, jnp.int32, jnp.bfloat16

    def plane(k):
        return {"slab": z * nd + lax.rem(d + k, nd)}

    def ring(step):
        return {"slab": lax.rem(z + step + nz, nz) * nd + d}

    def across(k):
        return {"rock": lax.rem(x + k + nx, nx)}

    def remote(src, dst, ss, rs, peer):
        return pltpu.make_async_remote_copy(
            src_ref=src, dst_ref=dst, send_sem=ss, recv_sem=rs, device_id=peer, device_id_type=MESH
        )

    def wait_bytes(ref, sem):
        pltpu.make_async_copy(ref, ref, sem).wait()

    peers = [plane(k) for k in range(1, nd)] + [ring(1), ring(-1), across(1), across(-1)]
    barrier = pltpu.get_barrier_semaphore()
    for peer in peers:
        pl.semaphore_signal(barrier, inc=1, device_id=peer, device_id_type=MESH)

    loads = [
        pltpu.make_async_copy(
            strain_hbm.at[c, :, pl.ds(lb * lanes, lanes)], strain.at[c, lb], load_s.at[c * blocks + lb]
        )
        for c in range(comps)
        for lb in range(blocks)
    ]
    for load in loads:
        load.start()
    load_res = pltpu.make_async_copy(res_hbm, res, load_s.at[comps * blocks])
    load_res.start()

    upper = lax.broadcasted_iota(i32, (2 * QDIR, lanes), 0) < QDIR
    upper_rows = lax.broadcasted_iota(i32, (2 * QDIR, owners), 0) < QDIR
    number = lax.broadcasted_iota(i32, (tiles, owners), 0)
    owner_of = lax.broadcasted_iota(i32, (tiles, owners), 1)
    slot_rows = []
    for a in range(ANGLES):
        named = jnp.broadcast_to(dest[pl.ds(a, 1), :].astype(f32), (owners, tiles)).T.astype(i32)
        falls = jnp.broadcast_to(det_row[pl.ds(a, 1), :].astype(f32), (owners, tiles)).T.astype(i32)
        key = number * ROWS + falls
        match = named == owner_of
        low = jnp.min(jnp.where(match, key, tiles * ROWS), axis=0, keepdims=True)
        high = jnp.max(jnp.where(match, key, -1), axis=0, keepdims=True)
        low = jnp.where(high >= 0, low, -1)
        high = jnp.where(high > low, high, -1)
        for slot, keys in enumerate((low, high)):
            idx_v[pl.ds(a * CAP + slot, 1), :] = lax.shift_right_logical(jnp.maximum(keys, 0), 3)
        low, high = [jnp.where(keys >= 0, keys & (ROWS - 1), -1).astype(f32) for keys in (low, high)]
        slot_rows.append(
            jnp.where(upper_rows, jnp.broadcast_to(low, upper_rows.shape), jnp.broadcast_to(high, upper_rows.shape))
        )
    idx_copy = pltpu.make_async_copy(idx_v, idx, idx_s)
    idx_copy.start()
    slot_rows = jnp.concatenate(slot_rows, axis=0).astype(bf16)
    source = lax.broadcasted_iota(i32, (owners, nz * ROWS), 0)
    target = lax.broadcasted_iota(i32, (owners, nz * ROWS), 1)
    row_of = (lax.broadcasted_iota(i32, (2 * ANGLES * QDIR, nz * ROWS), 1) & (ROWS - 1)).astype(f32)
    start_of = lax.shift_right_logical(target, 3) * nd
    for k in range(nd):
        spread = jnp.where(source == start_of + k, 1.0, 0.0).astype(bf16)
        there = jnp.dot(slot_rows, spread, preferred_element_type=f32)
        hot = jnp.where(there == row_of, 1.0, 0.0)
        for a in range(ANGLES):
            oh[k, a] = hot[a * 2 * QDIR : (a + 1) * 2 * QDIR]
    qs = lax.broadcasted_iota(i32, (2 * QDIR, lanes), 0) & (QDIR - 1)
    for a in range(ANGLES):
        for c in range(comps):
            column = jnp.full(qs.shape, dirs[a, 0, c])
            for q in range(1, QDIR):
                column = jnp.where(qs == q, dirs[a, q, c], column)
            w[a, c] = column * scale
    idx_copy.wait()
    for load in loads:
        load.wait()

    def dest_z(m, sign):
        off = half - m
        if sign == 0:
            return lax.rem(z + off, nz)
        back = lax.rem(off, half)
        return lax.rem(z - back + nz, nz)

    pl.semaphore_wait(barrier, len(peers))

    for k in range(1, nd):
        remote(oh.at[lax.rem(d + k, nd)], ohrecv.at[d], oh_ss, oh_rs, plane(k)).start()
    ohrecv[d] = oh[d]

    def pair(a, owner):
        first, second = idx[a * CAP, owner], idx[a * CAP + 1, owner]
        values = []
        for lb in range(blocks):
            total = None
            for c in range(comps):
                s0 = jnp.broadcast_to(strain[c, lb, pl.ds(first, 1), :], upper.shape)
                s1 = jnp.broadcast_to(strain[c, lb, pl.ds(second, 1), :], upper.shape)
                term = w[a, c] * jnp.where(upper, s0, s1)
                total = term if total is None else total + term
            values.append(total)
        return jnp.concatenate(values, axis=1)

    def send_group(a, m):
        for k in range(1, nd):
            dk = lax.rem(d + k, nd)
            for sign in range(2):
                ysend[a, m, k - 1, sign] = pair(a, dest_z(m, sign) * nd + dk)
            remote(
                ysend.at[a, m, k - 1], yrecv.at[a, m, d], y_ss.at[a, m], y_rs.at[a, m], plane(k)
            ).start()
        for sign in range(2):
            yrecv[a, m, d, sign] = pair(a, dest_z(m, sign) * nd + d)

    def need_group(a, m):
        wait_bytes(yrecv.at[a, m, pl.ds(0, nd - 1)], y_rs.at[a, m])

    def work(a, m, sign, g):
        zd = dest_z(m, sign)
        lhs = ohm[a, pl.ds(pl.multiple_of(zd * ROWS, ROWS), ROWS), :].astype(bf16)
        values = []
        for i in range(per):
            p = yrecv[a, m, :, sign].reshape(nd * 2 * QDIR, px)
            e = jnp.exp2(p * (ra[g * per + i] * (2.0 * scale) - p))
            hi = e.astype(bf16)
            lo = (e - hi.astype(f32)).astype(bf16)
            values.append(jnp.dot(lhs, jnp.concatenate([hi, lo], axis=0), preferred_element_type=f32))
        return values

    def z_step(a, m, g, way, has):
        here = zrecv.at[a, m - 1, way, g]
        values = work(a, m, way, g)
        if has:
            wait_bytes(here, z_rs.at[a, m - 1, way, g])
            values = [value + here[i] for i, value in enumerate(values)]
        for i, value in enumerate(values):
            here[i] = value
        remote(
            here, zrecv.at[a, m, way, g], z_ss.at[a, m, way, g], z_rs.at[a, m, way, g], ring(1 - 2 * way)
        ).start()

    def z_first(a):
        def go(g, carry):
            for way in range(2):
                at = g + way * GROUPS // 2
                for i, value in enumerate(work(a, 0, 0, at)):
                    zfirst[a, at, i] = value
                remote(
                    zfirst.at[a, at], zrecv.at[a, 0, way, at], z_ss.at[a, 0, way, at], z_rs.at[a, 0, way, at],
                    ring(1 - 2 * way),
                ).start()
            return carry

        lax.fori_loop(0, GROUPS // 2, go, 0)

    def z_second(a):
        for has in (False, True):

            def go(i, carry, has=has):
                for way in range(2):
                    g = i + (way if has else 1 - way) * (GROUPS // 2)
                    z_step(a, 1, g, way, has)
                return carry

            lax.fori_loop(0, GROUPS // 2, go, 0)

    def z_rest(a, m):
        def go(i, carry):
            for way in range(2):
                z_step(a, m, i, way, True)
            return carry

        lax.fori_loop(0, GROUPS, go, 0)

    def finish(a, g):
        values = work(a, 0, 1, g)
        for way in range(2):
            wait_bytes(zrecv.at[a, half - 1, way, g], z_rs.at[a, half - 1, way, g])
        for i, value in enumerate(values):
            angle = jnp.full((ROWS, px), ra[g * per + i]) * scale
            value = value + zrecv[a, half - 1, 0, g, i] + zrecv[a, half - 1, 1, g, i]
            ximg[a, g, x, i] = value * (jnp.exp2(-angle * angle) * norm)
        for way in range(2):
            remote(
                ximg.at[a, g, x], ximg.at[a, g, x], x_ss.at[a, g, way], x_rs.at[a, g, way], across(1 - 2 * way)
            ).start()

    def halves(a, g, at, way):
        return ximg.at[a, g, at, pl.ds(way * (per // 2), per // 2)]

    def forward(a, g):
        for way in range(2):
            at = lax.rem(x + nx - 1 + 2 * way, nx)
            wait_bytes(ximg.at[a, g, at], x_rs.at[a, g, way])
            part = halves(a, g, at, way)
            remote(part, part, x_ss.at[a, g, 2 + way], x_rs.at[a, g, 2 + way], across(1 - 2 * way)).start()

    def resolve(a, g):
        for way in range(2):
            wait_bytes(halves(a, g, lax.rem(x + 2, nx), way), x_rs.at[a, g, 2 + way])
        total = None
        for j in range(nx):
            image = ximg[a, g, j].reshape(per * ROWS, px)
            hi = image.astype(bf16)
            lo = (image - hi.astype(f32)).astype(bf16)
            both = jnp.dot(
                jnp.concatenate([hi, lo], axis=0), res[pl.ds(j * px, px), :], preferred_element_type=f32
            )
            part = both[: per * ROWS] + both[per * ROWS :]
            total = part if total is None else total + part
        out[a, pl.ds(g * per, per)] = total.reshape(per, ROWS, res.shape[1])

    def each(fn, a):
        def go(g, carry):
            fn(a, g)
            return carry

        lax.fori_loop(0, GROUPS, go, 0)

    lead = min(LEAD, half)

    def ahead_of(a, m):
        ahead = a * half + m + lead

        @pl.when(ahead < ANGLES * half)
        def _():
            send_group(lax.div(ahead, half), lax.rem(ahead, half))

    def early(t, carry):
        send_group(0, t)
        return carry

    lax.fori_loop(0, lead, early, 0)
    wait_bytes(ohrecv.at[pl.ds(0, nd - 1)], oh_rs)
    for a in range(ANGLES):
        columns = ohrecv[:, a].reshape(nd * 2 * QDIR, nz * ROWS)
        rows = columns.T
        ohm[a] = jnp.concatenate([rows, rows], axis=1)

    def steady(a):
        def go(m, carry):
            ahead_of(a, m)
            need_group(a, m)
            z_rest(a, m)
            return carry

        return go

    for a in range(ANGLES):
        for m in range(2):
            ahead_of(a, m)
            need_group(a, m)
            (z_first if m == 0 else z_second)(a)
        if a > 0:
            each(finish, a - 1)
        lax.fori_loop(2, half - 1, steady(a), 0)
        if a > 0:
            each(forward, a - 1)
        if half > 2:
            lax.fori_loop(half - 1, half, steady(a), 0)
        if a > 0:
            load_res.wait()
            each(resolve, a - 1)
    last = ANGLES - 1
    finish(last, 0)

    def tail(g, carry):
        finish(last, g)
        forward(last, g - 1)
        return carry

    lax.fori_loop(1, GROUPS, tail, 0)
    forward(last, GROUPS - 1)
    each(resolve, last)

    wait_bytes(ohrecv.at[pl.ds(0, nd - 1)], oh_ss)

    def drain(t, carry):
        a, m = lax.div(t, half), lax.rem(t, half)
        wait_bytes(ysend.at[a, m, pl.ds(0, nd - 1)], y_ss.at[a, m])
        return carry

    lax.fori_loop(0, ANGLES * half, drain, 0)
    for a in range(ANGLES):

        def drain_z(m, carry):
            for way in range(2):
                for g in range(GROUPS):
                    wait_bytes(zrecv.at[a, m, way, g], z_ss.at[a, m, way, g])
            return carry

        for way in range(2):
            for g in range(way * GROUPS // 2, (way + 1) * GROUPS // 2):
                wait_bytes(zrecv.at[a, 0, way, g], z_ss.at[a, 0, way, g])
        lax.fori_loop(1, half, drain_z, 0)
        for g in range(GROUPS):
            for way in range(2):
                wait_bytes(ximg.at[a, g, 0], x_ss.at[a, g, way])
                wait_bytes(halves(a, g, 0, way), x_ss.at[a, g, 2 + way])


def local(plane, strain, dest, det_row, dirs, rock_angles, resolution):
    nslab, nx = lax.axis_size("slab"), lax.axis_size("rock")
    nd, nz = plane, nslab // plane
    half = nz // 2
    tiles, comps, px = strain.shape
    out_px = resolution.shape[1]
    rocks = rock_angles.shape[0]
    per = rocks // GROUPS
    lanes = min(128, px)
    blocks = px // lanes
    norm = ROWS / (QDIR * DEPTH * TILES_DEV)

    smem = pl.BlockSpec(memory_space=pltpu.SMEM)
    vmem = pl.BlockSpec(memory_space=pltpu.VMEM)
    hbm = pl.BlockSpec(memory_space=pl.ANY)
    dma = pltpu.SemaphoreType.DMA
    f32 = jnp.float32
    image = (per, ROWS, px)
    resolved = pl.pallas_call(
        functools.partial(kernel, nz, nd, norm),
        out_shape=jax.ShapeDtypeStruct((ANGLES, rocks, ROWS, out_px), f32),
        in_specs=[smem, smem, vmem, vmem, hbm, hbm],
        out_specs=vmem,
        scratch_shapes=[
            pltpu.SMEM((ANGLES * CAP, nslab), jnp.int32),
            pltpu.VMEM((ANGLES * CAP, nslab), jnp.int32),
            pltpu.VMEM((ANGLES, comps, 2 * QDIR, lanes), f32),
            pltpu.VMEM((comps, blocks, tiles, lanes), f32),
            pltpu.VMEM(resolution.shape, resolution.dtype),
            pltpu.VMEM((nd, ANGLES, CAP * QDIR, nz * ROWS), f32),
            pltpu.VMEM((ANGLES, half, nd - 1, 2, 2 * QDIR, px), f32),
            pltpu.VMEM((ANGLES, half, nd, 2, 2 * QDIR, px), f32),
            pltpu.VMEM((nd, ANGLES, CAP * QDIR, nz * ROWS), f32),
            pltpu.VMEM((ANGLES, nz * ROWS, 2 * nd * 2 * QDIR), f32),
            pltpu.VMEM((ANGLES, GROUPS, *image), f32),
            pltpu.VMEM((ANGLES, half, 2, GROUPS, *image), f32),
            pltpu.VMEM((ANGLES, GROUPS, nx, *image), f32),
            dma((comps * blocks + 1,)),
            dma,
            dma,
            dma,
            dma((ANGLES, half)),
            dma((ANGLES, half)),
            dma((ANGLES, half, 2, GROUPS)),
            dma((ANGLES, half, 2, GROUPS)),
            dma((ANGLES, GROUPS, 4)),
            dma((ANGLES, GROUPS, 4)),
        ],
        compiler_params=pltpu.CompilerParams(collective_id=0, has_side_effects=True),
    )(
        rock_angles,
        dirs,
        dest.reshape(ANGLES, tiles),
        det_row,
        jnp.transpose(strain, (1, 0, 2)),
        resolution,
    )
    return jnp.swapaxes(resolved, 1, 2)


def solution(mesh):
    placed = (
        P("slab", None, "rock"),
        P(None, "slab", None),
        P(None, "slab"),
        P(),
        P(),
        P(None, "rock"),
    )
    return jax.shard_map(
        functools.partial(local, PLANE),
        mesh=mesh,
        in_specs=placed,
        out_specs=P(None, "slab", None, "rock"),
        check_vma=False,
    )
```

time: 143 us -> 126 us (0.88)
  Pallas kernels: 131 us -> 123 us
  local copies, waits for them, and re-layouts: 7.24 us -> 2.14 us
  other arithmetic: 4.36 us -> 0 us
    pallas_call x1, Pallas kernels: 131 us -> 123 us  [local(): pl.pallas_call(functools.partial(kernel, nz, nd, norm), out_shape=jax.Sha...]
    unnamed x3 -> x0, local copies, waits for them, and re-layouts: 2.3 us -> none
    mul x3 -> x0, other arithmetic: 1.95 us -> none  [the longest x1 1.26 us: local(): post = norm * jnp.exp2(-angles * angles)]
where the time goes in v2:
time: 126 us; the launch traced here: 125 us
  Pallas kernels  123 us (98%)
  local copies, waits for them, and re-layouts  2.14 us (2%)
    pallas_call x1, Pallas kernels, local(): pl.pallas_call(functools.partial(kernel, nz, nd, norm), out_shape=jax.Sha...  123 us

profile of v2, /device:TPU:24, one launch (start us, length us, event | category | flops | bytes accessed | tf_op | source)
XLA Modules:
  0.0 124.8 jit_solution(3518331443513851823)
XLA Ops:
  0.0 122.6 %shard_map.64 = f32[2,16,8,512]{3,2,1,0:T(8,128)} custom-call(f32[16]{0:T(128)} %ra.1, f32[2,4,6]{2,1,0:T(4,128)} %dirs.1, s32[2,128]{1,0:T(2,128)} %bitcast.5, s32[2,128]{1,0:T(2,128)} %det_row.1, f32[6,128,512]{2,1,0:T(8,128)} %bitcast.4, bf16[2048,512]{1,0:T(8,128)(2,1)} %res_hbm.1), custom_call_target="tpu_custom_call" | custom-call | tf_op jit(solution)/shard_map/pallas_call | solution.py:362
  122.6 2.1 %copy.7 = f32[2,8,16,512]{3,2,1,0:T(8,128)} copy(f32[2,8,16,512]{3,1,2,0:T(8,128)} %bitcast.3) | data formatting | bytes 1048576 | tf_op jit(solution)/shard_map/transpose | solution.py:401

commit v3 on v2

--- a/solution.py
+++ b/solution.py
@@ -16,15 +16,15 @@
 CAP = 2
 PLANE = 8
 GROUPS = 4
-LEAD = 3
+LEAD = 11
 MESH = pl.DeviceIdType.MESH
 
 
 def kernel(
     nz, nd, norm,
     ra, dirs, dest, det_row, strain_hbm, res_hbm, out,
-    idx, idx_v, w, strain, res, oh, ysend, yrecv, ohrecv, ohm, zfirst, zrecv, ximg,
-    load_s, idx_s, oh_ss, oh_rs, y_ss, y_rs, z_ss, z_rs, x_ss, x_rs,
+    idx, idx_v, w, strain, res, oh, ysend, yrecv, ohrecv, ohm, zleaf, zown, zoh, zrecv, ximg, summed,
+    load_s, idx_s, oh_ss, oh_rs, y_ss, y_rs, p_ss, p_rs, z_ss, z_rs, x_ss, x_rs,
 ):
     me = lax.axis_index("slab")
     x = lax.axis_index("rock")
@@ -35,7 +35,8 @@
     owners = nz * nd
     comps, blocks, tiles, lanes = strain.shape
     px = blocks * lanes
-    per = zfirst.shape[2]
+    per = zrecv.shape[4]
+    hp = px // 2
     scale = math.sqrt(0.5 * math.log2(math.e))
     f32, i32, bf16 = jnp.float32, jnp.int32, jnp.bfloat16
 
@@ -71,7 +72,6 @@
     for load in loads:
         load.start()
     load_res = pltpu.make_async_copy(res_hbm, res, load_s.at[comps * blocks])
-    load_res.start()
 
     upper = lax.broadcasted_iota(i32, (2 * QDIR, lanes), 0) < QDIR
     upper_rows = lax.broadcasted_iota(i32, (2 * QDIR, owners), 0) < QDIR
@@ -117,12 +117,11 @@
     for load in loads:
         load.wait()
 
+    for a in range(ANGLES):
+        summed[a] = jnp.zeros(summed.shape[1:], f32)
+
     def dest_z(m, sign):
-        off = half - m
-        if sign == 0:
-            return lax.rem(z + off, nz)
-        back = lax.rem(off, half)
-        return lax.rem(z - back + nz, nz)
+        return lax.rem(z + (half - m) * (1 - 2 * sign) + nz, nz)
 
     pl.semaphore_wait(barrier, len(peers))
 
@@ -143,79 +142,133 @@
             values.append(total)
         return jnp.concatenate(values, axis=1)
 
-    def send_group(a, m):
-        for k in range(1, nd):
-            dk = lax.rem(d + k, nd)
-            for sign in range(2):
-                ysend[a, m, k - 1, sign] = pair(a, dest_z(m, sign) * nd + dk)
-            remote(
-                ysend.at[a, m, k - 1], yrecv.at[a, m, d], y_ss.at[a, m], y_rs.at[a, m], plane(k)
-            ).start()
-        for sign in range(2):
-            yrecv[a, m, d, sign] = pair(a, dest_z(m, sign) * nd + d)
-
-    def need_group(a, m):
-        wait_bytes(yrecv.at[a, m, pl.ds(0, nd - 1)], y_rs.at[a, m])
-
-    def work(a, m, sign, g):
-        zd = dest_z(m, sign)
-        lhs = ohm[a, pl.ds(pl.multiple_of(zd * ROWS, ROWS), ROWS), :].astype(bf16)
+    def unit(n):
+        first = n < 3 * ANGLES
+        rest = jnp.maximum(n - 3 * ANGLES, 0)
+        a = jnp.where(first, lax.div(n, 3), lax.div(rest, nz - 3))
+        v = jnp.where(first, lax.rem(n, 3) + 1, lax.rem(rest, nz - 3) + 4)
+        return a, lax.div(v, 2), lax.rem(v, 2)
+
+    def send_part(n, k):
+        a, m, sign = unit(n)
+        there = ysend.at[a, m, sign, k]
+        there[...] = pair(a, dest_z(m, sign) * nd + lax.rem(d + k, nd))
+
+        @pl.when(k > 0)
+        def _():
+            remote(there, yrecv.at[a, m, sign, d], y_ss.at[a, m, sign], y_rs.at[a, m, sign], plane(k)).start()
+
+        @pl.when(k == 0)
+        def _():
+            pltpu.make_async_copy(there, yrecv.at[a, m, sign, d], y_rs.at[a, m, sign]).start()
+
+    def advance(t, i):
+        for j in range(2):
+            n = LEAD + 2 * t + j
+
+            @pl.when(n < ANGLES * nz)
+            def _():
+                for k in range(nd // GROUPS):
+                    send_part(n, i * (nd // GROUPS) + k)
+
+    def need(a, m, sign):
+        wait_bytes(yrecv.at[a, m, sign], y_rs.at[a, m, sign])
+
+    def lines(a, zd):
+        return ohm.at[a, pl.ds(pl.multiple_of(zd * ROWS, ROWS), ROWS), :]
+
+    def images(p_ref, hot, g):
+        lhs = hot[...].astype(bf16)
         values = []
         for i in range(per):
-            p = yrecv[a, m, :, sign].reshape(nd * 2 * QDIR, px)
+            p = p_ref[...].reshape(nd * 2 * QDIR, p_ref.shape[-1])
             e = jnp.exp2(p * (ra[g * per + i] * (2.0 * scale) - p))
             hi = e.astype(bf16)
             lo = (e - hi.astype(f32)).astype(bf16)
             values.append(jnp.dot(lhs, jnp.concatenate([hi, lo], axis=0), preferred_element_type=f32))
         return values
 
-    def z_step(a, m, g, way, has):
+    def work(a, m, sign, g):
+        return images(yrecv.at[a, m, sign], lines(a, dest_z(m, sign)), g)
+
+    def pass_on(a, way, kind, pairs):
+        for j, (src, dst) in enumerate(pairs):
+            remote(src, dst, p_ss.at[a, kind + j, way], p_rs.at[a, kind + j, way], ring(1 - 2 * way)).start()
+
+    def leaf(a):
+        need(a, 0, 1)
+        for way in range(2):
+            part = yrecv.at[a, 0, 1, :, :, pl.ds(way * hp, hp)]
+            pass_on(a, way, 0, [(part, zleaf.at[a, 0, way]), (lines(a, dest_z(0, 1)), zoh.at[a, 0, way])])
+
+    def second(a):
+        need(a, 1, 0)
+        need(a, 1, 1)
+        for way in range(2):
+            pass_on(
+                a, way, 2,
+                [(yrecv.at[a, 1, way], zown.at[a, way]), (lines(a, dest_z(1, way)), zoh.at[a, 1, way])],
+            )
+
+    def leaf_again(a):
+        for way in range(2):
+            wait_bytes(zleaf.at[a, 0, way], p_rs.at[a, 0, way])
+            wait_bytes(zoh.at[a, 0, way], p_rs.at[a, 1, way])
+            pass_on(
+                a, way, 4, [(zleaf.at[a, 0, way], zleaf.at[a, 1, way]), (zoh.at[a, 0, way], zoh.at[a, 2, way])]
+            )
+
+    def send_on(a, m, g, way, values):
         here = zrecv.at[a, m - 1, way, g]
-        values = work(a, m, way, g)
-        if has:
-            wait_bytes(here, z_rs.at[a, m - 1, way, g])
-            values = [value + here[i] for i, value in enumerate(values)]
         for i, value in enumerate(values):
             here[i] = value
         remote(
             here, zrecv.at[a, m, way, g], z_ss.at[a, m, way, g], z_rs.at[a, m, way, g], ring(1 - 2 * way)
         ).start()
 
-    def z_first(a):
+    def z_third(a):
         def go(g, carry):
+            advance(a * (half - 2), g)
             for way in range(2):
-                at = g + way * GROUPS // 2
-                for i, value in enumerate(work(a, 0, 0, at)):
-                    zfirst[a, at, i] = value
-                remote(
-                    zfirst.at[a, at], zrecv.at[a, 0, way, at], z_ss.at[a, 0, way, at], z_rs.at[a, 0, way, at],
-                    ring(1 - 2 * way),
-                ).start()
+                values = work(a, 2, way, g)
+                if_first = [(zown.at[a, way], 2), (zoh.at[a, 1, way], 3), (zleaf.at[a, 1, way], 4), (zoh.at[a, 2, way], 5)]
+
+                @pl.when(g == 0)
+                def _():
+                    for ref, kind in if_first:
+                        wait_bytes(ref, p_rs.at[a, kind, way])
+
+                near = images(zown.at[a, way], zoh.at[a, 1, way], g)
+                far = images(zleaf.at[a, 1, way], zoh.at[a, 2, way], g)
+                total = []
+                for one, two, three in zip(values, near, far):
+                    sides = [one[:, :hp] + two[:, :hp], one[:, hp:] + two[:, hp:]]
+                    sides[way] = sides[way] + three
+                    total.append(jnp.concatenate(sides, axis=1))
+                send_on(a, 2, g, way, total)
             return carry
 
-        lax.fori_loop(0, GROUPS // 2, go, 0)
-
-    def z_second(a):
-        for has in (False, True):
-
-            def go(i, carry, has=has):
-                for way in range(2):
-                    g = i + (way if has else 1 - way) * (GROUPS // 2)
-                    z_step(a, 1, g, way, has)
-                return carry
-
-            lax.fori_loop(0, GROUPS // 2, go, 0)
-
-    def z_rest(a, m):
+        lax.fori_loop(0, GROUPS, go, 0)
+
+    def z_step(a, m, g, way):
+        here = zrecv.at[a, m - 1, way, g]
+        values = work(a, m, way, g)
+        wait_bytes(here, z_rs.at[a, m - 1, way, g])
+        send_on(a, m, g, way, [value + here[i] for i, value in enumerate(values)])
+
+    def z_rest(a, m, extra=None):
         def go(i, carry):
+            advance(a * (half - 2) + m - 2, i)
             for way in range(2):
-                z_step(a, m, i, way, True)
+                z_step(a, m, i, way)
+            if extra is not None:
+                extra(i)
             return carry
 
         lax.fori_loop(0, GROUPS, go, 0)
 
     def finish(a, g):
-        values = work(a, 0, 1, g)
+        values = work(a, half, 0, g)
         for way in range(2):
             wait_bytes(zrecv.at[a, half - 1, way, g], z_rs.at[a, half - 1, way, g])
         for i, value in enumerate(values):
@@ -237,20 +290,41 @@
             part = halves(a, g, at, way)
             remote(part, part, x_ss.at[a, g, 2 + way], x_rs.at[a, g, 2 + way], across(1 - 2 * way)).start()
 
-    def resolve(a, g):
+    def split(image):
+        hi = image.astype(bf16)
+        return jnp.concatenate([hi, (image - hi.astype(f32)).astype(bf16)], axis=0)
+
+    def far(a, g):
         for way in range(2):
             wait_bytes(halves(a, g, lax.rem(x + 2, nx), way), x_rs.at[a, g, 2 + way])
+
+    def columns_of(j):
+        return res[pl.ds(pl.multiple_of(j * px, px), px), :]
+
+    def resolve_block(a, j):
+        rows = per * GROUPS * ROWS
+        both = jnp.dot(split(ximg[a, :, j].reshape(rows, px)), columns_of(j), preferred_element_type=f32)
+        part = both[:rows] + both[rows:]
+        for lb in range(blocks):
+            summed[a, lb] += part[:, lb * lanes : (lb + 1) * lanes]
+
+    def resolve_group(a, g):
+        rows = per * ROWS
         total = None
-        for j in range(nx):
-            image = ximg[a, g, j].reshape(per * ROWS, px)
-            hi = image.astype(bf16)
-            lo = (image - hi.astype(f32)).astype(bf16)
-            both = jnp.dot(
-                jnp.concatenate([hi, lo], axis=0), res[pl.ds(j * px, px), :], preferred_element_type=f32
-            )
-            part = both[: per * ROWS] + both[per * ROWS :]
+        for k in (0, 1, 3, 2):
+            j = lax.rem(x + k, nx)
+            if k == 2:
+                far(a, g)
+            both = jnp.dot(split(ximg[a, g, j].reshape(rows, px)), columns_of(j), preferred_element_type=f32)
+            part = both[:rows] + both[rows:]
             total = part if total is None else total + part
-        out[a, pl.ds(g * per, per)] = total.reshape(per, ROWS, res.shape[1])
+        for lb in range(blocks):
+            summed[a, lb, pl.ds(pl.multiple_of(g * rows, rows), rows), :] = total[:, lb * lanes : (lb + 1) * lanes]
+
+    def deliver(a):
+        for row in range(ROWS):
+            for lb in range(blocks):
+                out[a, row, :, pl.ds(lb * lanes, lanes)] = summed[a, lb, pl.ds(row, per * GROUPS, stride=ROWS), :]
 
     def each(fn, a):
         def go(g, carry):
@@ -259,51 +333,63 @@
 
         lax.fori_loop(0, GROUPS, go, 0)
 
-    lead = min(LEAD, half)
-
-    def ahead_of(a, m):
-        ahead = a * half + m + lead
-
-        @pl.when(ahead < ANGLES * half)
-        def _():
-            send_group(lax.div(ahead, half), lax.rem(ahead, half))
-
-    def early(t, carry):
-        send_group(0, t)
+    def early(n, carry):
+        def go(k, inner):
+            send_part(n, k)
+            return inner
+
+        lax.fori_loop(0, nd, go, 0)
         return carry
 
-    lax.fori_loop(0, lead, early, 0)
+    lax.fori_loop(0, 3, early, 0)
+    load_res.start()
     wait_bytes(ohrecv.at[pl.ds(0, nd - 1)], oh_rs)
     for a in range(ANGLES):
         columns = ohrecv[:, a].reshape(nd * 2 * QDIR, nz * ROWS)
         rows = columns.T
         ohm[a] = jnp.concatenate([rows, rows], axis=1)
 
-    def steady(a):
+    def steady(a, extra=None):
         def go(m, carry):
-            ahead_of(a, m)
-            need_group(a, m)
-            z_rest(a, m)
+            need(a, m, 0)
+            need(a, m, 1)
+            z_rest(a, m, extra)
             return carry
 
         return go
 
+    leaf(0)
+    lax.fori_loop(3, 6, early, 0)
+    second(0)
+    lax.fori_loop(6, 8, early, 0)
+    leaf_again(0)
+    leaf(1)
+    lax.fori_loop(8, LEAD, early, 0)
+    second(1)
+    leaf_again(1)
+    cut = half // 2
     for a in range(ANGLES):
-        for m in range(2):
-            ahead_of(a, m)
-            need_group(a, m)
-            (z_first if m == 0 else z_second)(a)
+        need(a, 2, 0)
+        need(a, 2, 1)
+        z_third(a)
         if a > 0:
+            need(a - 1, half, 0)
             each(finish, a - 1)
-        lax.fori_loop(2, half - 1, steady(a), 0)
+        lax.fori_loop(3, cut, steady(a), 0)
         if a > 0:
             each(forward, a - 1)
-        if half > 2:
-            lax.fori_loop(half - 1, half, steady(a), 0)
+            load_res.wait()
+        lax.fori_loop(cut, half - 2, steady(a), 0)
+        extra = None
         if a > 0:
-            load_res.wait()
-            each(resolve, a - 1)
+            each(far, a - 1)
+            extra = lambda j, a=a: resolve_block(a - 1, j)
+        lax.fori_loop(half - 2, half - 1, steady(a, extra), 0)
+        lax.fori_loop(half - 1, half, steady(a), 0)
+        if a > 0:
+            deliver(a - 1)
     last = ANGLES - 1
+    need(last, half, 0)
     finish(last, 0)
 
     def tail(g, carry):
@@ -312,17 +398,24 @@
         return carry
 
     lax.fori_loop(1, GROUPS, tail, 0)
+    resolve_group(last, 0)
     forward(last, GROUPS - 1)
-    each(resolve, last)
+
+    def rest(g, carry):
+        resolve_group(last, g)
+        return carry
+
+    lax.fori_loop(1, GROUPS, rest, 0)
+    deliver(last)
 
     wait_bytes(ohrecv.at[pl.ds(0, nd - 1)], oh_ss)
 
-    def drain(t, carry):
-        a, m = lax.div(t, half), lax.rem(t, half)
-        wait_bytes(ysend.at[a, m, pl.ds(0, nd - 1)], y_ss.at[a, m])
+    def drain(n, carry):
+        a, m, sign = unit(n)
+        wait_bytes(ysend.at[a, m, sign, pl.ds(0, nd - 1)], y_ss.at[a, m, sign])
         return carry
 
-    lax.fori_loop(0, ANGLES * half, drain, 0)
+    lax.fori_loop(0, ANGLES * nz, drain, 0)
     for a in range(ANGLES):
 
         def drain_z(m, carry):
@@ -332,9 +425,11 @@
             return carry
 
         for way in range(2):
-            for g in range(way * GROUPS // 2, (way + 1) * GROUPS // 2):
-                wait_bytes(zrecv.at[a, 0, way, g], z_ss.at[a, 0, way, g])
-        lax.fori_loop(1, half, drain_z, 0)
+            for kind, ref in enumerate(
+                (zleaf.at[a, 0, way], zoh.at[a, 0, way], zown.at[a, way], zoh.at[a, 0, way], zleaf.at[a, 0, way], zoh.at[a, 0, way])
+            ):
+                wait_bytes(ref, p_ss.at[a, kind, way])
+        lax.fori_loop(2, half, drain_z, 0)
         for g in range(GROUPS):
             for way in range(2):
                 wait_bytes(ximg.at[a, g, 0], x_ss.at[a, g, way])
@@ -361,7 +456,7 @@
     image = (per, ROWS, px)
     resolved = pl.pallas_call(
         functools.partial(kernel, nz, nd, norm),
-        out_shape=jax.ShapeDtypeStruct((ANGLES, rocks, ROWS, out_px), f32),
+        out_shape=jax.ShapeDtypeStruct((ANGLES, ROWS, rocks, out_px), f32),
         in_specs=[smem, smem, vmem, vmem, hbm, hbm],
         out_specs=vmem,
         scratch_shapes=[
@@ -371,19 +466,24 @@
             pltpu.VMEM((comps, blocks, tiles, lanes), f32),
             pltpu.VMEM(resolution.shape, resolution.dtype),
             pltpu.VMEM((nd, ANGLES, CAP * QDIR, nz * ROWS), f32),
-            pltpu.VMEM((ANGLES, half, nd - 1, 2, 2 * QDIR, px), f32),
-            pltpu.VMEM((ANGLES, half, nd, 2, 2 * QDIR, px), f32),
+            pltpu.VMEM((ANGLES, half + 1, 2, nd, 2 * QDIR, px), f32),
+            pltpu.VMEM((ANGLES, half + 1, 2, nd, 2 * QDIR, px), f32),
             pltpu.VMEM((nd, ANGLES, CAP * QDIR, nz * ROWS), f32),
             pltpu.VMEM((ANGLES, nz * ROWS, 2 * nd * 2 * QDIR), f32),
-            pltpu.VMEM((ANGLES, GROUPS, *image), f32),
+            pltpu.VMEM((ANGLES, 2, 2, nd, 2 * QDIR, px // 2), f32),
+            pltpu.VMEM((ANGLES, 2, nd, 2 * QDIR, px), f32),
+            pltpu.VMEM((ANGLES, 3, 2, ROWS, 2 * nd * 2 * QDIR), f32),
             pltpu.VMEM((ANGLES, half, 2, GROUPS, *image), f32),
             pltpu.VMEM((ANGLES, GROUPS, nx, *image), f32),
+            pltpu.VMEM((ANGLES, blocks, rocks * ROWS, lanes), f32),
             dma((comps * blocks + 1,)),
             dma,
             dma,
             dma,
-            dma((ANGLES, half)),
-            dma((ANGLES, half)),
+            dma((ANGLES, half + 1, 2)),
+            dma((ANGLES, half + 1, 2)),
+            dma((ANGLES, 6, 2)),
+            dma((ANGLES, 6, 2)),
             dma((ANGLES, half, 2, GROUPS)),
             dma((ANGLES, half, 2, GROUPS)),
             dma((ANGLES, GROUPS, 4)),
@@ -398,7 +498,7 @@
         jnp.transpose(strain, (1, 0, 2)),
         resolution,
     )
-    return jnp.swapaxes(resolved, 1, 2)
+    return resolved
 
 
 def solution(mesh):

time: 126 us -> 118 us (0.937)
  Pallas kernels: 123 us -> 116 us
    pallas_call x1, Pallas kernels: 123 us -> 116 us  [local(): pl.pallas_call(functools.partial(kernel, nz, nd, norm), out_shape=jax.Sha...]
    transpose x1 -> x0, local copies, waits for them, and re-layouts: 2.14 us -> none  [local(): return jnp.swapaxes(resolved, 1, 2)]
    unnamed x0 -> x1, local copies, waits for them, and re-layouts: none -> 1.88 us
where the time goes in v3:
time: 118 us
  Pallas kernels  116 us (98%)
  local copies, waits for them, and re-layouts  1.88 us (2%)
    pallas_call x1, Pallas kernels, local(): pl.pallas_call(functools.partial(kernel, nz, nd, norm), out_shape=jax.Sha...  116 us

profile of v3, /device:TPU:24, one launch (start us, length us, event | category | flops | bytes accessed | tf_op | source)
XLA Modules:
  0.0 117.9 jit_solution(6148176065724392989)
XLA Ops:
  0.0 116.0 %shard_map.64 = f32[2,8,16,512]{3,2,1,0:T(8,128)} custom-call(f32[16]{0:T(128)} %ra.1, f32[2,4,6]{2,1,0:T(4,128)} %dirs.1, s32[2,128]{1,0:T(2,128)} %bitcast.3, s32[2,128]{1,0:T(2,128)} %det_row.1, f32[6,128,512]{2,1,0:T(8,128)} %bitcast.2, bf16[2048,512]{1,0:T(8,128)(2,1)} %res_hbm.1), custom_call_target="tpu_custom_call" | custom-call | tf_op jit(solution)/shard_map/pallas_call | solution.py:457
  116.0 1.9 %copy.8 = f32[2,8,16,512]{3,2,1,0:T(8,128)} copy(f32[2,8,16,512]{3,2,1,0:T(8,128)} %shard_map.64) | data formatting | bytes 1048576
